TPU v7x, 128 devices: a whole 4x4x4 slice. The times are simulated.
128 devices in a mesh: cols: 2 (over core), patch: 64 (over x, y, z).
Axes of the slice: x: 4, y: 4, z: 4, core: 2. Of those that a mesh axis runs over, the one named last changes fastest.
Arguments:
- vectors: bfloat16 [262144, 512], P('patch', 'cols'), may hold values from -6 to 6
- blocks: bfloat16 [2048, 8, 128, 128], P('patch'), may hold values from -0.09375 to 0.09375
- tile_cols: int32 [2048, 8], P('patch'), may hold values from 0 to 2047, as said below
- live_tiles: int32 [64], P('patch'), may hold values from 1 to 32, as said below
Outputs:
- result: bfloat16 [262144, 512], P('patch', 'cols')
Inputs may be any that keep to these rules, and one draw needn't show every extreme that they name: `tile_cols`: each listed tile lies within 4 tiles of its own tile row; entries may repeat, and repeated blocks add. `live_tiles`: some patch is full in every draw.
All inputs are finite; a program needn't handle non-finite values.
Results may differ from a plain program's by a relative error of at most 0.0064.
Values may be sent and summed in bfloat16 or wider, within the bound.
A program may use at most 128 MiB of HBM per device.

v0:
```python
import functools

import jax
import jax.numpy as jnp
from jax import lax
from jax.experimental import pallas as pl
from jax.experimental.pallas import tpu as pltpu
from jax.sharding import PartitionSpec as P

MESH = pl.DeviceIdType.MESH
F32, BF16 = jnp.float32, jnp.bfloat16
TILE = 128
HALO = 4
STEPS = 3
ITERS = 8
RING = 4
SPLIT = 2


def tdot(a, b):
    return lax.dot_general(a, b, (((0,), (0,)), ((), ())), preferred_element_type=F32)


def filter_kernel(
    n_patch, cols, live, vec, blk_hbm, own_out, par_out, gram_out,
    raw, blk, ys, los, his, par, acc, pay, rsb, zb, gb,
    in_sem, blk_sem, halo_send, halo_recv, swap_send, swap_recv,
    rs_send, rs_recv, z_send, z_recv, ag_send, ag_recv, gx_send, gx_recv, out_sem,
):
    tiles, width = raw.shape[0], raw.shape[2]
    part = width // SPLIT
    core, me = lax.axis_index("cols"), lax.axis_index("patch")
    planes = n_patch // RING
    plane, z = me // RING, me % RING
    right, left = (me + 1) % n_patch, (me + n_patch - 1) % n_patch

    def plane_peer(d):
        return ((plane + d) % planes) * RING + z

    def z_peer(d):
        return plane * RING + (z + d) % RING

    def patch(index):
        return {"patch": index}

    def send(src, dst, ssem, rsem, target):
        return pltpu.make_async_remote_copy(
            src_ref=src, dst_ref=dst, send_sem=ssem, recv_sem=rsem,
            device_id=target, device_id_type=MESH,
        )

    edge = 2 * HALO
    mid = tiles - 2 * edge
    loads = [
        pltpu.make_async_copy(vec.at[pl.ds(s, n)], raw.at[pl.ds(s, n)], in_sem.at[i])
        for i, (s, n) in enumerate(((0, edge), (tiles - edge, edge), (edge, mid)))
    ]
    for copy in loads:
        copy.start()
    blk_loads = [
        pltpu.make_async_copy(blk_hbm.at[pl.ds(s, HALO)], blk.at[pl.ds(s, HALO)], blk_sem.at[i])
        for i, s in enumerate(range(0, tiles, HALO))
    ]
    for copy in blk_loads:
        copy.start()

    barrier = pltpu.get_barrier_semaphore()
    targets = [patch(right), patch(left), {"cols": 1 - core}]
    targets += [patch(plane_peer(d)) for d in range(1, planes)]
    targets += [patch(z_peer(d)) for d in range(1, RING)]
    for target in targets:
        pl.semaphore_signal(barrier, inc=1, device_id=target, device_id_type=MESH)

    def weight(t):
        return (t < live[0]).astype(F32)

    def keep(k, t, value):
        ys[k][t] = value

    def edges(k, t, slot, side):
        for h in range(SPLIT):
            side[k][h][slot] = ys[k][t, :, h * part : (h + 1) * part]

    def mask(start, count):
        def body(i, _):
            t = start + i
            ys[0][t] = (raw[t].astype(F32) * weight(t)).astype(BF16)
            return 0

        lax.fori_loop(0, count, body, 0)

    loads[0].wait()
    mask(0, edge)
    loads[1].wait()
    mask(tiles - edge, edge)

    def copy_edges(k, first, count):
        for i in range(count):
            t = first + i
            side, slot = (los, t + HALO) if t < edge else (his, t - (tiles - edge))
            edges(k, t, slot, side)

    copy_edges(0, 0, edge)
    copy_edges(0, tiles - edge, edge)
    pl.semaphore_wait(barrier, len(targets))

    def halo(k, h):
        return (
            send(
                los[k][h].at[pl.ds(HALO, HALO)], his[k][h].at[pl.ds(2 * HALO, HALO)],
                halo_send.at[k, h, 0], halo_recv.at[k, h, 0], patch(left),
            ),
            send(
                his[k][h].at[pl.ds(HALO, HALO)], los[k][h].at[pl.ds(0, HALO)],
                halo_send.at[k, h, 1], halo_recv.at[k, h, 1], patch(right),
            ),
        )

    halos = {}
    for h in range(SPLIT):
        halos[0, h] = halo(0, h)
        for copy in halos[0, h]:
            copy.start()

    loads[2].wait()
    mask(edge, mid)
    for copy in blk_loads:
        copy.wait()

    def product(k, t, source, base, lanes):
        shift = me * tiles + base
        lhs = jnp.concatenate([blk[t, n] for n in range(blk.shape[1])], axis=1)
        slots = [jnp.clip(cols[n, t] - shift, 0, source.shape[0] - 1) for n in range(blk.shape[1])]
        rhs = jnp.concatenate([source[slot] for slot in slots], axis=0)
        total = jnp.dot(lhs, rhs, preferred_element_type=F32)
        if k > 1:
            total = 2.0 * total - ys[k - 2][t, :, lanes].astype(F32)
        return (total * weight(t)).astype(BF16)

    def inner(k, start, count):
        def body(i, _):
            t = start + i
            ys[k][t] = product(k, t, ys[k - 1], 0, slice(None))
            return 0

        lax.fori_loop(0, count, body, 0)

    def outer(k, h):
        lanes = slice(h * part, (h + 1) * part)

        def low(t, _):
            value = product(k, t, los[k - 1][h], -HALO, lanes)
            ys[k][t, :, lanes] = value
            if k < STEPS:
                los[k][h][t + HALO] = value
            return 0

        def high(i, _):
            t = tiles - HALO + i
            value = product(k, t, his[k - 1][h], tiles - edge, lanes)
            ys[k][t, :, lanes] = value
            if k < STEPS:
                his[k][h][i + HALO] = value
            return 0

        halos[k - 1, h][1].wait_recv()
        lax.fori_loop(0, HALO, low, 0)
        halos[k - 1, h][0].wait_recv()
        lax.fori_loop(0, HALO, high, 0)

    swaps = []

    def swap(start, count):
        i = len(swaps)
        copy = send(
            ys[STEPS].at[pl.ds(start, count)], par.at[pl.ds(start, count)],
            swap_send.at[i], swap_recv.at[i], {"cols": 1 - core},
        )
        copy.start()
        swaps.append(copy)

    for k in range(1, STEPS + 1):
        inner(k, HALO * k, tiles - 2 * HALO * k)
    copy_edges(1, HALO, HALO)
    copy_edges(1, tiles - edge, HALO)
    swap(HALO * STEPS, tiles - 2 * HALO * STEPS)

    def gram(start, count, step):
        def body(i, _):
            rows = pl.ds(start + i * step, step)
            mine = ys[STEPS][rows].reshape(step * TILE, width)
            other = par[rows].reshape(step * TILE, width)
            acc[:, :width] += tdot(mine, mine)
            acc[:, width:] += tdot(mine, other)
            return 0

        lax.fori_loop(0, count // step, body, 0)

    acc[...] = jnp.zeros_like(acc)
    for k in range(1, STEPS + 1):
        for h in range(SPLIT):
            outer(k, h)
            if k < STEPS:
                halos[k, h] = halo(k, h)
                for copy in halos[k, h]:
                    copy.start()
        for later in range(k + 1, STEPS + 1):
            near = HALO * (later - k)
            for start in (near, tiles - HALO - near):
                inner(later, start, HALO)
                if later == k + 1 and later < STEPS:
                    copy_edges(later, start, HALO)
                if later == STEPS:
                    swap(start, HALO)
        if k == STEPS - 1:
            for copy in swaps:
                copy.wait_recv()
            gram(HALO, tiles - 2 * HALO, edge)
    early = len(swaps)
    swap(0, HALO)
    swap(tiles - HALO, HALO)
    own_copy = pltpu.make_async_copy(ys[STEPS], own_out, out_sem.at[0])
    own_copy.start()
    for copy in swaps[early:]:
        copy.wait_recv()
    par_copy = pltpu.make_async_copy(par, par_out, out_sem.at[1])
    par_copy.start()
    gram(0, HALO, HALO)
    gram(tiles - HALO, HALO, HALO)

    own = acc[:, :width]
    first = core == 0
    cross = [acc[i * TILE : (i + 1) * TILE, width:] for i in range(2)]
    chunk = pay.shape[1]
    blocks = (
        own[:TILE, :TILE],
        own[:TILE, TILE:],
        own[TILE:, TILE:],
        jnp.where(first, cross[0][:, :TILE], cross[0][:, TILE:]),
        jnp.where(first, cross[1][:, TILE:], cross[1][:, :TILE]),
    )
    flat = jnp.concatenate(blocks, axis=0).reshape(pay.shape)
    pay[...] = flat

    scatter = []
    for d in range(1, planes):
        copy = send(
            pay.at[(plane + d) % planes], rsb.at[d], rs_send.at[d], rs_recv.at[d],
            patch(plane_peer(d)),
        )
        copy.start()
        scatter.append(copy)
    total = pay[plane]
    for d in range(1, planes):
        scatter[d - 1].wait_recv()
        total = total + rsb[d]
    zb[z] = total
    along = []
    for d in range(1, RING):
        copy = send(zb.at[z], zb.at[z], z_send.at[d], z_recv.at[d], patch(z_peer(d)))
        copy.start()
        along.append(copy)
    for copy in along:
        copy.wait_recv()
    total = zb[0]
    for d in range(1, RING):
        total = total + zb[d]
    for copy in along:
        copy.wait_send()
    gb[core, plane] = total
    gather = []
    for d in range(1, planes):
        copy = send(
            gb.at[core, plane], gb.at[core, plane], ag_send.at[d], ag_recv.at[d],
            patch(plane_peer(d)),
        )
        copy.start()
        gather.append(copy)
    for copy in gather:
        copy.wait_recv()
    cross_copy = send(gb.at[core], gb.at[core], gx_send, gx_recv, {"cols": 1 - core})
    cross_copy.start()
    cross_copy.wait_recv()
    gram_copy = pltpu.make_async_copy(gb, gram_out, out_sem.at[2])
    gram_copy.start()

    for copies in halos.values():
        for copy in copies:
            copy.wait_send()
    for copy in swaps + scatter + gather + [cross_copy]:
        copy.wait_send()
    own_copy.wait()
    par_copy.wait()
    gram_copy.wait()


def filtered_and_gram(n_patch, vectors, blocks, listed, live):
    tiles, _, width = vectors.shape
    nnz = blocks.shape[1]
    planes = n_patch // RING
    chunk = 5 * TILE // planes
    part = width // SPLIT
    any_space = pl.BlockSpec(memory_space=pl.ANY)
    smem = pl.BlockSpec(memory_space=pltpu.SMEM)
    dma = pltpu.SemaphoreType.DMA
    side = [[pltpu.VMEM((3 * HALO, TILE, part), BF16) for _ in range(SPLIT)] for _ in range(STEPS)]
    swaps = 2 * STEPS + 1
    return pl.pallas_call(
        functools.partial(filter_kernel, n_patch),
        out_shape=(
            jax.ShapeDtypeStruct((tiles, TILE, width), BF16),
            jax.ShapeDtypeStruct((tiles, TILE, width), BF16),
            jax.ShapeDtypeStruct((2, planes, chunk, TILE), F32),
        ),
        in_specs=[smem, smem, any_space, any_space],
        out_specs=(any_space, any_space, any_space),
        scratch_shapes=[
            pltpu.VMEM((tiles, TILE, width), BF16),
            pltpu.VMEM((tiles, nnz, TILE, TILE), BF16),
            [pltpu.VMEM((tiles, TILE, width), BF16) for _ in range(STEPS + 1)],
            side,
            side,
            pltpu.VMEM((tiles, TILE, width), BF16),
            pltpu.VMEM((width, 2 * width), F32),
            pltpu.VMEM((planes, chunk, TILE), F32),
            pltpu.VMEM((planes, chunk, TILE), F32),
            pltpu.VMEM((RING, chunk, TILE), F32),
            pltpu.VMEM((2, planes, chunk, TILE), F32),
            dma((3,)),
            dma((tiles // HALO,)),
            dma((STEPS, SPLIT, 2)),
            dma((STEPS, SPLIT, 2)),
            dma((swaps,)),
            dma((swaps,)),
            dma((planes,)),
            dma((planes,)),
            dma((RING,)),
            dma((RING,)),
            dma((planes,)),
            dma((planes,)),
            dma,
            dma,
            dma((3,)),
        ],
        compiler_params=pltpu.CompilerParams(
            collective_id=0, has_side_effects=True, vmem_limit_bytes=60 * 2**20
        ),
        name="filter_gram",
    )(listed, live, vectors, blocks)


def rotate_kernel(
    rows_total, gram, own_hbm, par_hbm, out_hbm, full, xh, xl, zmat, zh, zl, own, par, out, in_sem, out_sem
):
    width = own.shape[2]
    size = 2 * width
    tiles = own.shape[0]
    core = lax.axis_index("cols")
    loads = [
        pltpu.make_async_copy(own_hbm, own, in_sem.at[0]),
        pltpu.make_async_copy(par_hbm, par, in_sem.at[1]),
    ]
    for copy in loads:
        copy.start()

    piece = lambda c, i: gram[c, i * TILE : (i + 1) * TILE, :]

    def put(i, j, value):
        full[i * TILE : (i + 1) * TILE, j * TILE : (j + 1) * TILE] = value
        if i != j:
            full[j * TILE : (j + 1) * TILE, i * TILE : (i + 1) * TILE] = value.T

    for c in range(2):
        put(2 * c, 2 * c, piece(c, 0))
        put(2 * c, 2 * c + 1, piece(c, 1))
        put(2 * c + 1, 2 * c + 1, piece(c, 2))
    put(0, 2, piece(0, 3))
    put(1, 3, piece(0, 4))
    put(2, 1, piece(1, 3))
    put(3, 0, piece(1, 4))

    g = full[...]
    norm = jnp.sqrt(jnp.sum(g * g))
    x = g / norm
    eye = (
        lax.broadcasted_iota(jnp.int32, (size, size), 0)
        == lax.broadcasted_iota(jnp.int32, (size, size), 1)
    ).astype(F32)
    full[...] = 1.5 * eye - 0.5 * x
    zmat[...] = full[:, pl.ds(pl.multiple_of(core * width, width), width)]

    def split(value, high, low):
        h = value.astype(BF16)
        high[...] = h
        low[...] = (value - h.astype(F32)).astype(BF16)

    full[...] = x
    split(x, xh, xl)

    def times(high, low, yh, yl):
        dot = functools.partial(jnp.dot, preferred_element_type=F32)
        return dot(high, yh) + (dot(high, yl) + dot(low, yh))

    def advance(_, carry):
        high, low = xh[...], xl[...]
        square = times(high, low, high, low)
        sh = square.astype(BF16)
        sl = (square - sh.astype(F32)).astype(BF16)
        value = 2.25 * full[...] - 1.5 * square + 0.25 * times(high, low, sh, sl)
        full[...] = value
        split(value, xh, xl)
        return carry

    def turn(_, carry):
        split(zmat[...], zh, zl)
        zmat[...] = 1.5 * zmat[...] - 0.5 * times(xh[...], xl[...], zh[...], zl[...])
        return carry

    advance(0, 0)

    def both(i, carry):
        turn(i, carry)
        return advance(i, carry)

    lax.fori_loop(1, ITERS - 1, both, 0)
    turn(0, 0)

    factor = jnp.sqrt(rows_total / norm)
    zh[...] = zmat[...].astype(BF16)
    top = zh[pl.ds(pl.multiple_of(core * width, width), width), :]
    low = zh[pl.ds(pl.multiple_of((1 - core) * width, width), width), :]
    for copy in loads:
        copy.wait()
    group = 4
    stores = []

    def rows(i, carry):
        at = pl.ds(i * group, group)
        a = own[at].reshape(group * TILE, width)
        b = par[at].reshape(group * TILE, width)
        value = jnp.dot(a, top, preferred_element_type=F32) + jnp.dot(b, low, preferred_element_type=F32)
        out[at] = (value * factor).astype(BF16).reshape(group, TILE, width)
        pltpu.make_async_copy(out.at[at], out_hbm.at[at], out_sem.at[i]).start()
        return carry

    lax.fori_loop(0, tiles // group, rows, 0)
    for i in range(tiles // group):
        at = pl.ds(i * group, group)
        pltpu.make_async_copy(out.at[at], out_hbm.at[at], out_sem.at[i]).wait()


def rotated(rows_total, gram, own, par):
    tiles, _, width = own.shape
    size = 2 * width
    any_space = pl.BlockSpec(memory_space=pl.ANY)
    vmem = pl.BlockSpec(memory_space=pltpu.VMEM)
    dma = pltpu.SemaphoreType.DMA
    return pl.pallas_call(
        functools.partial(rotate_kernel, rows_total),
        out_shape=jax.ShapeDtypeStruct(own.shape, BF16),
        in_specs=[vmem, any_space, any_space],
        out_specs=any_space,
        scratch_shapes=[
            pltpu.VMEM((size, size), F32),
            pltpu.VMEM((size, size), BF16),
            pltpu.VMEM((size, size), BF16),
            pltpu.VMEM((size, width), F32),
            pltpu.VMEM((size, width), BF16),
            pltpu.VMEM((size, width), BF16),
            pltpu.VMEM((tiles, TILE, width), BF16),
            pltpu.VMEM((tiles, TILE, width), BF16),
            pltpu.VMEM((tiles, TILE, width), BF16),
            dma((2,)),
            dma((tiles // 4,)),
        ],
        compiler_params=pltpu.CompilerParams(vmem_limit_bytes=60 * 2**20),
        name="rotate",
    )(gram, own, par)


def on_device(vectors, blocks, tile_cols, live_tiles):
    tiles, width = blocks.shape[0], vectors.shape[1]
    n_patch = lax.axis_size("patch")
    own, par, gram = filtered_and_gram(
        n_patch, vectors.reshape(tiles, TILE, width), blocks, tile_cols.T, live_tiles
    )
    result = rotated(n_patch * tiles * TILE, gram.reshape(2, -1, TILE), own, par)
    return result.reshape(tiles * TILE, width)


def solution(mesh):
    in_specs = (P("patch", "cols"), P("patch", None, None, None), P("patch", None), P("patch"))
    out_specs = P("patch", "cols")
    return jax.shard_map(
        on_device, mesh=mesh, in_specs=in_specs, out_specs=out_specs, check_vma=False
    )
```

profile of v0, /device:TPU:1, one launch (start us, length us, event | category | flops | bytes accessed | tf_op | source)
XLA Modules:
  0.0 96.0 jit_solution(7747793327929668757)
XLA Ops:
  0.7 65.7 %filter_gram.1 = (bf16[32,128,256]{2,1,0:T(8,128)(2,1)}, bf16[32,128,256]{2,1,0:T(8,128)(2,1)}, f32[2,16,40,128]{3,2,1,0:T(8,128)}) custom-call(s32[8,32]{1,0:T(8,128)} %bitcast.6, s32[1]{0:T(128)S(6)} %copy.5.live, bf16[32,128,256]{2,1,0:T(8,128)(2,1)} %bitcast.4, bf16[32,8,128,128]{3,2,1,0:T(8,128)(2,1)} %blk_hbm.1), custom_call_target="tpu_custom_call" | custom-call | tf_op jit(solution)/shard_map/filter_gram/pallas_call | solution.py:308
  66.4 29.6 %rotate.1 = bf16[32,128,256]{2,1,0:T(8,128)(2,1)} custom-call(f32[2,640,128]{2,1,0:T(8,128)} %bitcast.5, bf16[32,128,256]{2,1,0:T(8,128)(2,1)} %get-tuple-element.9.own_hbm, bf16[32,128,256]{2,1,0:T(8,128)(2,1)} %get-tuple-element.10.par_hbm), custom_call_target="tpu_custom_call" | custom-call | tf_op jit(solution)/shard_map/rotate/pallas_call | solution.py:458
where the time goes:
time: 96.2 us; the launch traced here: 96 us
  Pallas kernels  95.3 us (99%)
    pallas_call x1, Pallas kernels, filtered_and_gram(): pl.pallas_call(functools.partial(filter_kernel, n_patch), out_shape=(jax....  65.7 us
    pallas_call x1, Pallas kernels, rotated(): pl.pallas_call(functools.partial(rotate_kernel, rows_total), out_shape=ja...  29.6 us

commit v1 on v0

--- a/solution.py
+++ b/solution.py
@@ -104,23 +104,21 @@
     copy_edges(0, tiles - edge, edge)
     pl.semaphore_wait(barrier, len(targets))
 
-    def halo(k, h):
-        return (
-            send(
-                los[k][h].at[pl.ds(HALO, HALO)], his[k][h].at[pl.ds(2 * HALO, HALO)],
-                halo_send.at[k, h, 0], halo_recv.at[k, h, 0], patch(left),
-            ),
-            send(
-                his[k][h].at[pl.ds(HALO, HALO)], los[k][h].at[pl.ds(0, HALO)],
-                halo_send.at[k, h, 1], halo_recv.at[k, h, 1], patch(right),
-            ),
+    halos = {}
+
+    def launch(k, h, up):
+        mine, theirs = (his, los) if up else (los, his)
+        copy = send(
+            mine[k][h].at[pl.ds(HALO, HALO)],
+            theirs[k][h].at[pl.ds(0 if up else 2 * HALO, HALO)],
+            halo_send.at[k, h, int(up)], halo_recv.at[k, h, int(up)], patch(right if up else left),
         )
-
-    halos = {}
+        copy.start()
+        halos[k, h, up] = copy
+
     for h in range(SPLIT):
-        halos[0, h] = halo(0, h)
-        for copy in halos[0, h]:
-            copy.start()
+        for up in (True, False):
+            launch(0, h, up)
 
     loads[2].wait()
     mask(edge, mid)
@@ -139,34 +137,26 @@
 
     def inner(k, start, count):
         def body(i, _):
-            t = start + i
-            ys[k][t] = product(k, t, ys[k - 1], 0, slice(None))
+            for j in range(HALO):
+                t = start + i * HALO + j
+                ys[k][t] = product(k, t, ys[k - 1], 0, slice(None))
             return 0
 
-        lax.fori_loop(0, count, body, 0)
+        lax.fori_loop(0, count // HALO, body, 0)
 
     def outer(k, h):
         lanes = slice(h * part, (h + 1) * part)
-
-        def low(t, _):
-            value = product(k, t, los[k - 1][h], -HALO, lanes)
-            ys[k][t, :, lanes] = value
+        for up in ((False, True) if k % 2 else (True, False)):
+            side, slot = (his, tiles - edge) if up else (los, -HALO)
+            halos[k - 1, h, not up].wait_recv()
+            for i in range(HALO):
+                t = tiles - HALO + i if up else i
+                value = product(k, t, side[k - 1][h], slot, lanes)
+                ys[k][t, :, lanes] = value
+                if k < STEPS:
+                    side[k][h][i + HALO] = value
             if k < STEPS:
-                los[k][h][t + HALO] = value
-            return 0
-
-        def high(i, _):
-            t = tiles - HALO + i
-            value = product(k, t, his[k - 1][h], tiles - edge, lanes)
-            ys[k][t, :, lanes] = value
-            if k < STEPS:
-                his[k][h][i + HALO] = value
-            return 0
-
-        halos[k - 1, h][1].wait_recv()
-        lax.fori_loop(0, HALO, low, 0)
-        halos[k - 1, h][0].wait_recv()
-        lax.fori_loop(0, HALO, high, 0)
+                launch(k, h, up)
 
     swaps = []
 
@@ -200,10 +190,6 @@
     for k in range(1, STEPS + 1):
         for h in range(SPLIT):
             outer(k, h)
-            if k < STEPS:
-                halos[k, h] = halo(k, h)
-                for copy in halos[k, h]:
-                    copy.start()
         for later in range(k + 1, STEPS + 1):
             near = HALO * (later - k)
             for start in (near, tiles - HALO - near):
@@ -276,18 +262,20 @@
         )
         copy.start()
         gather.append(copy)
-    for copy in gather:
+    across = []
+    for d in range(planes):
+        if d > 0:
+            gather[d - 1].wait_recv()
+        at = (plane + planes - d) % planes
+        copy = send(gb.at[core, at], gb.at[core, at], gx_send.at[d], gx_recv.at[d], {"cols": 1 - core})
+        copy.start()
+        across.append(copy)
+    for copy in across:
         copy.wait_recv()
-    cross_copy = send(gb.at[core], gb.at[core], gx_send, gx_recv, {"cols": 1 - core})
-    cross_copy.start()
-    cross_copy.wait_recv()
     gram_copy = pltpu.make_async_copy(gb, gram_out, out_sem.at[2])
     gram_copy.start()
 
-    for copies in halos.values():
-        for copy in copies:
-            copy.wait_send()
-    for copy in swaps + scatter + gather + [cross_copy]:
+    for copy in list(halos.values()) + swaps + scatter + gather + across:
         copy.wait_send()
     own_copy.wait()
     par_copy.wait()
@@ -338,8 +326,8 @@
             dma((RING,)),
             dma((planes,)),
             dma((planes,)),
-            dma,
-            dma,
+            dma((planes,)),
+            dma((planes,)),
             dma((3,)),
         ],
         compiler_params=pltpu.CompilerParams(
@@ -350,7 +338,7 @@
 
 
 def rotate_kernel(
-    rows_total, gram, own_hbm, par_hbm, out_hbm, full, xh, xl, zmat, zh, zl, own, par, out, in_sem, out_sem
+    rows_total, gram, own_hbm, par_hbm, out_hbm, full, xh, xl, sh, sl, zmat, zh, zl, own, par, out, in_sem, out_sem
 ):
     width = own.shape[2]
     size = 2 * width
@@ -381,52 +369,73 @@
 
     g = full[...]
     norm = jnp.sqrt(jnp.sum(g * g))
-    x = g / norm
-    eye = (
-        lax.broadcasted_iota(jnp.int32, (size, size), 0)
-        == lax.broadcasted_iota(jnp.int32, (size, size), 1)
+    x = g * (1.0 / norm)
+    full[...] = x
+
+    def split(value):
+        high = value.astype(BF16)
+        return high, (value - high.astype(F32)).astype(BF16)
+
+    xh[...], xl[...] = split(x)
+    start = 1.5 * (
+        lax.broadcasted_iota(jnp.int32, (size, width), 0)
+        == lax.broadcasted_iota(jnp.int32, (size, width), 1) + core * width
     ).astype(F32)
-    full[...] = 1.5 * eye - 0.5 * x
-    zmat[...] = full[:, pl.ds(pl.multiple_of(core * width, width), width)]
-
-    def split(value, high, low):
-        h = value.astype(BF16)
-        high[...] = h
-        low[...] = (value - h.astype(F32)).astype(BF16)
-
-    full[...] = x
-    split(x, xh, xl)
-
-    def times(high, low, yh, yl):
+    z = start - 0.5 * full[:, pl.ds(pl.multiple_of(core * width, width), width)]
+    zmat[...] = z
+    zh[...], zl[...] = split(z)
+
+    def times(count, ah, al, bh, bl, lanes):
         dot = functools.partial(jnp.dot, preferred_element_type=F32)
-        return dot(high, yh) + (dot(high, yl) + dot(low, yh))
-
-    def advance(_, carry):
-        high, low = xh[...], xl[...]
-        square = times(high, low, high, low)
-        sh = square.astype(BF16)
-        sl = (square - sh.astype(F32)).astype(BF16)
-        value = 2.25 * full[...] - 1.5 * square + 0.25 * times(high, low, sh, sl)
-        full[...] = value
-        split(value, xh, xl)
+        high = ah[:count, :]
+        both = dot(jnp.concatenate([high, al[:count, :]], axis=0), bh[:, lanes])
+        return both[:count] + (both[count:] + dot(high, bl[:, lanes]))
+
+    halves = [slice(i * width, (i + 1) * width) for i in range(2)]
+
+    def keep(high, low, i, j, value):
+        h, l = split(value)
+        high[halves[i], halves[j]] = h
+        low[halves[i], halves[j]] = l
+        if i != j:
+            high[halves[j], halves[i]] = h.T
+            low[halves[j], halves[i]] = l.T
+
+    upper = ((0, 0), (0, 1), (1, 1))
+
+    def square():
+        for j in (1, 0):
+            s = times((j + 1) * width, xh, xl, xh, xl, halves[j])
+            rows = slice(0, (j + 1) * width)
+            full[rows, halves[j]] = 2.25 * full[rows, halves[j]] - 1.5 * s
+            for i in range(j + 1):
+                keep(sh, sl, i, j, s[halves[i]])
+
+    def cube():
+        for j in (1, 0):
+            rows = slice(0, (j + 1) * width)
+            p = times((j + 1) * width, xh, xl, sh, sl, halves[j])
+            full[rows, halves[j]] = full[rows, halves[j]] + 0.25 * p
+        for i, j in upper:
+            keep(xh, xl, i, j, full[halves[i], halves[j]])
+
+    def turn():
+        zmat[...] = 1.5 * zmat[...] - 0.5 * times(size, xh, xl, zh, zl, slice(None))
+        zh[...], zl[...] = split(zmat[...])
+
+    square()
+    cube()
+
+    def both(i, carry):
+        square()
+        turn()
+        cube()
         return carry
 
-    def turn(_, carry):
-        split(zmat[...], zh, zl)
-        zmat[...] = 1.5 * zmat[...] - 0.5 * times(xh[...], xl[...], zh[...], zl[...])
-        return carry
-
-    advance(0, 0)
-
-    def both(i, carry):
-        turn(i, carry)
-        return advance(i, carry)
-
     lax.fori_loop(1, ITERS - 1, both, 0)
-    turn(0, 0)
+    turn()
 
     factor = jnp.sqrt(rows_total / norm)
-    zh[...] = zmat[...].astype(BF16)
     top = zh[pl.ds(pl.multiple_of(core * width, width), width), :]
     low = zh[pl.ds(pl.multiple_of((1 - core) * width, width), width), :]
     for copy in loads:
@@ -464,6 +473,8 @@
             pltpu.VMEM((size, size), F32),
             pltpu.VMEM((size, size), BF16),
             pltpu.VMEM((size, size), BF16),
+            pltpu.VMEM((size, size), BF16),
+            pltpu.VMEM((size, size), BF16),
             pltpu.VMEM((size, width), F32),
             pltpu.VMEM((size, width), BF16),
             pltpu.VMEM((size, width), BF16),

time: 96.2 us -> 77.2 us (0.80)
  Pallas kernels: 95.3 us -> 76.4 us
    pallas_call x1, Pallas kernels: 29.6 us -> 19 us  [rotated(): pl.pallas_call(functools.partial(rotate_kernel, rows_total), out_shape=ja...]
    pallas_call x1, Pallas kernels: 65.7 us -> 57.3 us  [filtered_and_gram(): pl.pallas_call(functools.partial(filter_kernel, n_patch), out_shape=(jax....]
where the time goes in v1:
time: 77.2 us; the launch traced here: 77 us
  Pallas kernels  76.4 us (99%)
    pallas_call x1, Pallas kernels, filtered_and_gram(): pl.pallas_call(functools.partial(filter_kernel, n_patch), out_shape=(jax....  57.3 us
    pallas_call x1, Pallas kernels, rotated(): pl.pallas_call(functools.partial(rotate_kernel, rows_total), out_shape=ja...  19 us

profile of v1, /device:TPU:1, one launch (start us, length us, event | category | flops | bytes accessed | tf_op | source)
XLA Modules:
  0.0 77.0 jit_solution(12056542666656225014)
XLA Ops:
  0.7 57.3 %filter_gram.1 = (bf16[32,128,256]{2,1,0:T(8,128)(2,1)}, bf16[32,128,256]{2,1,0:T(8,128)(2,1)}, f32[2,16,40,128]{3,2,1,0:T(8,128)}) custom-call(s32[8,32]{1,0:T(8,128)} %bitcast.6, s32[1]{0:T(128)S(6)} %copy.5.live, bf16[32,128,256]{2,1,0:T(8,128)(2,1)} %bitcast.4, bf16[32,8,128,128]{3,2,1,0:T(8,128)(2,1)} %blk_hbm.1), custom_call_target="tpu_custom_call" | custom-call | tf_op jit(solution)/shard_map/filter_gram/pallas_call | solution.py:296
  58.0 19.0 %rotate.1 = bf16[32,128,256]{2,1,0:T(8,128)(2,1)} custom-call(f32[2,640,128]{2,1,0:T(8,128)} %bitcast.5, bf16[32,128,256]{2,1,0:T(8,128)(2,1)} %get-tuple-element.9.own_hbm, bf16[32,128,256]{2,1,0:T(8,128)(2,1)} %get-tuple-element.10.par_hbm), custom_call_target="tpu_custom_call" | custom-call | tf_op jit(solution)/shard_map/rotate/pallas_call | solution.py:467

commit v2 on v1

v2 whole, which is shorter than its diff:
```python
import functools

import jax
import jax.numpy as jnp
from jax import lax
from jax.experimental import pallas as pl
from jax.experimental.pallas import tpu as pltpu
from jax.sharding import PartitionSpec as P

MESH = pl.DeviceIdType.MESH
F32, BF16 = jnp.float32, jnp.bfloat16
TILE = 128
HALO = 4
STEPS = 3
ITERS = 8
RING = 4
PIECES = 2
SPLIT = 2


def tdot(a, b):
    return lax.dot_general(a, b, (((0,), (0,)), ((), ())), preferred_element_type=F32)


def pack_gram(own, other, first, pay):
    row = lax.broadcasted_iota(jnp.int32, (TILE, TILE), 0)
    lane = lax.broadcasted_iota(jnp.int32, (TILE, TILE), 1)
    last = own[TILE:, TILE:]
    blocks = (
        jnp.where(row <= lane, own[:TILE, :TILE], last),
        own[:TILE, TILE:],
        jnp.where(first, other[:TILE, :TILE], other[:TILE, TILE:]),
        jnp.where(first, other[TILE:, TILE:], other[TILE:, :TILE]),
    )
    chunks = pay.shape[0]
    rows = 4 * TILE // chunks
    pay[:, :rows, :] = jnp.concatenate(blocks, axis=0).reshape(chunks, rows, TILE)
    line = jnp.sum(jnp.where(row == lane, last, 0.0), axis=0, keepdims=True)
    per = TILE // chunks
    for q in range(chunks):
        pay[q, rows:, :] = jnp.where(lane[:1] // per == q, line, 0.0)


def filter_kernel(
    n_patch, cols, live, vec, blk_hbm, own_out, par_out, gram_out,
    raw, blk, ys, los, his, par, acc, pay, rsb, zb, gb,
    in_sem, blk_sem, halo_send, halo_recv, swap_send, swap_recv,
    rs_send, rs_recv, z_send, z_recv, ag_send, ag_recv, gx_send, gx_recv, out_sem,
):
    tiles, width = raw.shape[0], raw.shape[2]
    part = width // SPLIT
    core, me = lax.axis_index("cols"), lax.axis_index("patch")
    planes = n_patch // RING
    plane, z = lax.div(me, RING), lax.rem(me, RING)
    px, py = lax.div(plane, RING), lax.rem(plane, RING)
    right, left = lax.rem(me + 1, n_patch), lax.rem(me + n_patch - 1, n_patch)

    def far(d):
        return sum(min(v, RING - v) for v in divmod(d, RING))

    offsets = sorted(range(1, planes), key=far, reverse=True)

    def plane_at(dx, dy):
        return lax.rem(px + dx, RING) * RING + lax.rem(py + dy, RING)

    peer_plane = {d: plane_at(*divmod(d, RING)) for d in offsets}
    source_plane = {d: plane_at(*((RING - v) % RING for v in divmod(d, RING))) for d in offsets}

    def plane_peer(d):
        return peer_plane[d] * RING + z

    def z_peer(d):
        return plane * RING + lax.rem(z + d, RING)

    def patch(index):
        return {"patch": index}

    def send(src, dst, ssem, rsem, target):
        return pltpu.make_async_remote_copy(
            src_ref=src, dst_ref=dst, send_sem=ssem, recv_sem=rsem,
            device_id=target, device_id_type=MESH,
        )

    edge = 2 * HALO
    mid = tiles - 2 * edge
    spans = ((0, HALO), (tiles - HALO, HALO), (HALO, HALO), (tiles - edge, HALO), (edge, mid))
    loads = [
        pltpu.make_async_copy(vec.at[pl.ds(s, n)], raw.at[pl.ds(s, n)], in_sem.at[i])
        for i, (s, n) in enumerate(spans)
    ]
    for copy in loads[:2]:
        copy.start()
    barrier = pltpu.get_barrier_semaphore()
    targets = [patch(right), patch(left), {"cols": 1 - core}]
    targets += [patch(plane_peer(d)) for d in offsets]
    targets += [patch(z_peer(d)) for d in range(1, RING)]
    for target in targets:
        pl.semaphore_signal(barrier, inc=1, device_id=target, device_id_type=MESH)
    for copy in loads[2:]:
        copy.start()
    blk_loads = [
        pltpu.make_async_copy(blk_hbm.at[pl.ds(s, HALO)], blk.at[pl.ds(s, HALO)], blk_sem.at[i])
        for i, s in enumerate(range(0, tiles, HALO))
    ]
    for copy in blk_loads[1:] + blk_loads[:1]:
        copy.start()

    def weight(t):
        return (t < live[0]).astype(F32)

    def beside(k, t, value, h, lanes):
        if t < edge:
            los[k][h][t + HALO] = value[:, lanes]
        elif t >= tiles - edge:
            his[k][h][t - (tiles - edge)] = value[:, lanes]

    lanes_of = [slice(h * part, (h + 1) * part) for h in range(SPLIT)]

    def mask(t):
        value = (raw[t].astype(F32) * weight(t)).astype(BF16)
        ys[0][t] = value
        return value

    def mask_end(start):
        for t in range(start, start + HALO):
            value = mask(t)
            for h in range(SPLIT):
                beside(0, t, value, h, lanes_of[h])

    halos = {}
    half = HALO // PIECES

    def linked(up):
        return pl.when(me != n_patch - 1) if up else pl.when(me != 0)

    @pl.when(me == 0)
    def _():
        for k in range(STEPS):
            for h in range(SPLIT):
                los[k][h][:HALO] = jnp.zeros((HALO, TILE, part), BF16)

    @pl.when(me == n_patch - 1)
    def _():
        for k in range(STEPS):
            for h in range(SPLIT):
                his[k][h][2 * HALO :] = jnp.zeros((HALO, TILE, part), BF16)

    def launch(k, h, up, p):
        mine, theirs = (his, los) if up else (los, his)
        copy = send(
            mine[k][h].at[pl.ds(HALO + p * half, half)],
            theirs[k][h].at[pl.ds((0 if up else 2 * HALO) + p * half, half)],
            halo_send.at[k, h, int(up), p], halo_recv.at[k, h, int(up), p], patch(right if up else left),
        )
        linked(up)(copy.start)
        halos[k, h, up, p] = copy

    loads[0].wait()
    mask_end(0)
    loads[1].wait()
    mask_end(tiles - HALO)
    pl.semaphore_wait(barrier, len(targets))
    for h in range(SPLIT):
        for up in (True, False):
            for p in range(PIECES):
                launch(0, h, up, p)
    loads[2].wait()
    mask_end(HALO)
    loads[3].wait()
    mask_end(tiles - edge)
    loads[4].wait()

    def mask_mid(i, _):
        for j in range(HALO):
            mask(edge + i * HALO + j)
        return 0

    lax.fori_loop(0, mid // HALO, mask_mid, 0)

    def product(k, t, source, base, lanes):
        shift = me * tiles + base
        lhs = jnp.concatenate([blk[t, n] for n in range(blk.shape[1])], axis=1)
        slots = [jnp.clip(cols[n, t] - shift, 0, source.shape[0] - 1) for n in range(blk.shape[1])]
        rhs = jnp.concatenate([source[slot] for slot in slots], axis=0)
        total = jnp.dot(lhs, rhs, preferred_element_type=F32)
        if k > 1:
            total = 2.0 * total - ys[k - 2][t, :, lanes].astype(F32)
        return (total * weight(t)).astype(BF16)

    def inner(k, start, count, loading=False):
        def body(i, _):
            first = start + i * HALO
            if loading:
                rows = pl.ds(first, HALO)
                pltpu.make_async_copy(blk_hbm.at[rows], blk.at[rows], blk_sem.at[lax.div(first, HALO)]).wait()
            for j in range(HALO):
                t = first + j
                ys[k][t] = product(k, t, ys[k - 1], 0, slice(None))
            return 0

        lax.fori_loop(0, count // HALO, body, 0)

    swaps = []

    def swap(start, count, lanes):
        i = len(swaps)
        copy = send(
            ys[STEPS].at[pl.ds(start, count), :, lanes], par.at[pl.ds(start, count), :, lanes],
            swap_send.at[i], swap_recv.at[i], {"cols": 1 - core},
        )
        copy.start()
        swaps.append(copy)

    every = slice(0, width)

    def copy_ends(k, first):
        for t in range(first, first + HALO):
            for h in range(SPLIT):
                beside(k, t, ys[k][t], h, lanes_of[h])

    def outer(k, h):
        for up in ((False, True) if k % 2 else (True, False)):
            side, slot = (his, tiles - edge) if up else (los, -HALO)
            first = tiles - HALO if up else 0
            for p in range(PIECES):
                linked(up)(halos[k - 1, h, not up, p].wait_recv)
            for p in range(PIECES):
                for t in range(first + p * half, first + (p + 1) * half):
                    value = product(k, t, side[k - 1][h], slot, lanes_of[h])
                    ys[k][t, :, lanes_of[h]] = value
                    if k < STEPS:
                        beside(k, t, value, h, slice(None))
                if k < STEPS:
                    launch(k, h, up, p)
            if k == STEPS:
                swap(first, HALO, lanes_of[h])

    inner(1, HALO, tiles - 2 * HALO, loading=True)
    for copy in (blk_loads[0], blk_loads[-1]):
        copy.wait()
    copy_ends(1, HALO)
    copy_ends(1, tiles - edge)
    inner(2, 2 * HALO, tiles - 4 * HALO)

    def gram(start, count, step):
        def body(i, _):
            rows = pl.ds(start + i * step, step)
            mine = ys[STEPS][rows].reshape(step * TILE, width)
            other = par[rows].reshape(step * TILE, width)
            acc[:, :width] += tdot(mine, mine)
            acc[:, width:] += tdot(mine, other)
            return 0

        lax.fori_loop(0, count // step, body, 0)

    acc[...] = jnp.zeros_like(acc)
    for k in range(1, STEPS + 1):
        for h in range(SPLIT):
            outer(k, h)
        if k == 1:
            inner(STEPS, HALO * STEPS, tiles - 2 * HALO * STEPS)
            swap(HALO * STEPS, tiles - 2 * HALO * STEPS, every)
        for later in range(k + 1, STEPS + 1):
            near = HALO * (later - k)
            for start in (near, tiles - HALO - near):
                inner(later, start, HALO)
                if later == k + 1 and later < STEPS:
                    copy_ends(later, start)
                if later == STEPS:
                    swap(start, HALO, every)
        if k == STEPS - 1:
            early = len(swaps)
            for copy in swaps:
                copy.wait_recv()
            gram(HALO, tiles - 2 * HALO, edge)
    own_copy = pltpu.make_async_copy(ys[STEPS], own_out, out_sem.at[0])
    own_copy.start()

    def ends(ref):
        rows = [ref[pl.ds(s, HALO)].reshape(HALO * TILE, width) for s in (0, tiles - HALO)]
        return jnp.concatenate(rows, axis=0)

    mine = ends(ys[STEPS])
    acc[:, :width] += tdot(mine, mine)
    for copy in swaps[early:]:
        copy.wait_recv()
    par_copy = pltpu.make_async_copy(par, par_out, out_sem.at[1])
    par_copy.start()
    acc[:, width:] += tdot(ends(ys[STEPS]), ends(par))
    pack_gram(acc[:, :width], acc[:, width:], core == 0, pay)

    scatter = []
    for d in offsets:
        copy = send(pay.at[peer_plane[d]], rsb.at[d], rs_send.at[d], rs_recv.at[d], patch(plane_peer(d)))
        copy.start()
        scatter.append(copy)
    total = pay[plane]
    for d, copy in zip(offsets[::-1], scatter[::-1]):
        copy.wait_recv()
        total = total + rsb[d]
    zb[z] = total
    along = []
    for d in range(1, RING):
        copy = send(zb.at[z], zb.at[z], z_send.at[d], z_recv.at[d], patch(z_peer(d)))
        copy.start()
        along.append(copy)
    for copy in along:
        copy.wait_recv()
    total = zb[0]
    for d in range(1, RING):
        total = total + zb[d]
    for copy in along:
        copy.wait_send()
    gb[core, plane] = total
    gather = []
    for d in offsets:
        copy = send(
            gb.at[core, plane], gb.at[core, plane], ag_send.at[d], ag_recv.at[d], patch(plane_peer(d))
        )
        copy.start()
        gather.append(copy)
    across = []

    def cross(d, at):
        copy = send(gb.at[core, at], gb.at[core, at], gx_send.at[d], gx_recv.at[d], {"cols": 1 - core})
        copy.start()
        across.append(copy)

    cross(0, plane)
    for d, copy in zip(offsets[::-1], gather[::-1]):
        copy.wait_recv()
        cross(d, source_plane[d])
    for copy in across:
        copy.wait_recv()
    gram_copy = pltpu.make_async_copy(gb, gram_out, out_sem.at[2])
    gram_copy.start()

    for (k, h, up, p), copy in halos.items():
        linked(up)(copy.wait_send)
    for copy in swaps + scatter + gather + across:
        copy.wait_send()
    own_copy.wait()
    par_copy.wait()
    gram_copy.wait()


def filtered_and_gram(n_patch, vectors, blocks, listed, live):
    tiles, _, width = vectors.shape
    nnz = blocks.shape[1]
    planes = n_patch // RING
    chunk = 4 * TILE // planes + 1
    part = width // SPLIT
    any_space = pl.BlockSpec(memory_space=pl.ANY)
    hbm = pl.BlockSpec(memory_space=pltpu.HBM)
    smem = pl.BlockSpec(memory_space=pltpu.SMEM)
    dma = pltpu.SemaphoreType.DMA
    side = [[pltpu.VMEM((3 * HALO, TILE, part), BF16) for _ in range(SPLIT)] for _ in range(STEPS)]
    swaps = 2 * STEPS - 1 + 2 * SPLIT
    return pl.pallas_call(
        functools.partial(filter_kernel, n_patch),
        out_shape=(
            jax.ShapeDtypeStruct((tiles, TILE, width), BF16),
            jax.ShapeDtypeStruct((tiles, TILE, width), BF16),
            jax.ShapeDtypeStruct((2, planes, chunk, TILE), F32),
        ),
        in_specs=[smem, smem, hbm, hbm],
        out_specs=(any_space, any_space, any_space),
        scratch_shapes=[
            pltpu.VMEM((tiles, TILE, width), BF16),
            pltpu.VMEM((tiles, nnz, TILE, TILE), BF16),
            [pltpu.VMEM((tiles, TILE, width), BF16) for _ in range(STEPS + 1)],
            side,
            side,
            pltpu.VMEM((tiles, TILE, width), BF16),
            pltpu.VMEM((width, 2 * width), F32),
            pltpu.VMEM((planes, chunk, TILE), F32),
            pltpu.VMEM((planes, chunk, TILE), F32),
            pltpu.VMEM((RING, chunk, TILE), F32),
            pltpu.VMEM((2, planes, chunk, TILE), F32),
            dma((5,)),
            dma((tiles // HALO,)),
            dma((STEPS, SPLIT, 2, PIECES)),
            dma((STEPS, SPLIT, 2, PIECES)),
            dma((swaps,)),
            dma((swaps,)),
            dma((planes,)),
            dma((planes,)),
            dma((RING,)),
            dma((RING,)),
            dma((planes,)),
            dma((planes,)),
            dma((planes,)),
            dma((planes,)),
            dma((3,)),
        ],
        compiler_params=pltpu.CompilerParams(
            collective_id=0, has_side_effects=True, vmem_limit_bytes=48 * 2**20
        ),
        name="filter_gram",
    )(listed, live, vectors, blocks)


def rotate_kernel(
    rows_total, gram, own_hbm, par_hbm, out_hbm, full, xh, xl, sh, sl, zmat, zh, zl, own, par, out, in_sem, out_sem
):
    width = own.shape[2]
    size = 2 * width
    tiles = own.shape[0]
    core = lax.axis_index("cols")
    loads = [
        pltpu.make_async_copy(own_hbm, own, in_sem.at[0]),
        pltpu.make_async_copy(par_hbm, par, in_sem.at[1]),
    ]
    for copy in loads:
        copy.start()

    row = lax.broadcasted_iota(jnp.int32, (TILE, TILE), 0)
    lane = lax.broadcasted_iota(jnp.int32, (TILE, TILE), 1)
    per = gram.shape[1] // 4

    def piece(c, i):
        return gram[c, i * per : (i + 1) * per, : TILE // per, :].reshape(TILE, TILE)

    blocks = {}
    for c in range(2):
        mixed, line = piece(c, 0), jnp.sum(gram[c, :, TILE // per :, :], axis=0)
        turned = mixed.T
        blocks[2 * c, 2 * c] = jnp.where(row <= lane, mixed, turned)
        blocks[2 * c + 1, 2 * c + 1] = jnp.where(row > lane, mixed, jnp.where(row < lane, turned, line))
        blocks[2 * c, 2 * c + 1] = piece(c, 1)
    blocks[0, 2], blocks[1, 3] = piece(0, 2), piece(0, 3)
    blocks[2, 1], blocks[3, 0] = piece(1, 2), piece(1, 3)
    total = sum((1.0 if i == j else 2.0) * jnp.sum(v * v, axis=0, keepdims=True) for (i, j), v in blocks.items())
    norm = jnp.sqrt(jnp.sum(total))
    inv = 1.0 / norm

    def put(i, j, value):
        full[i * TILE : (i + 1) * TILE, j * TILE : (j + 1) * TILE] = value

    for (i, j), value in blocks.items():
        value = value * inv
        if i <= j:
            put(i, j, value)
        if i > j or (i, j) in ((0, 1), (2, 3)):
            put(j, i, value.T)

    def split(value):
        high = value.astype(BF16)
        return high, (value - high.astype(F32)).astype(BF16)

    halves = [slice(i * width, (i + 1) * width) for i in range(2)]
    upper = ((0, 0), (0, 1), (1, 1))

    def keep(high, low, i, j, value):
        h, l = split(value)
        high[halves[i], halves[j]] = h
        low[halves[i], halves[j]] = l
        if i != j:
            high[halves[j], halves[i]] = h.T
            low[halves[j], halves[i]] = l.T

    for i, j in upper:
        keep(xh, xl, i, j, full[halves[i], halves[j]])
    mine = pl.ds(pl.multiple_of(core * width, width), width)
    eye = (
        lax.broadcasted_iota(jnp.int32, (size, width), 0)
        == lax.broadcasted_iota(jnp.int32, (size, width), 1) + core * width
    )
    z = jnp.where(eye, 1.5, 0.0) - 0.5 * (xh[:, mine].astype(F32) + xl[:, mine].astype(F32))
    zmat[...] = z
    zh[...], zl[...] = split(z)

    def times(count, ah, al, bh, bl, lanes):
        dot = functools.partial(jnp.dot, preferred_element_type=F32)
        high = ah[:count, :]
        both = dot(jnp.concatenate([high, al[:count, :]], axis=0), bh[:, lanes])
        return both[:count] + (both[count:] + dot(high, bl[:, lanes]))

    def square():
        for j in (1, 0):
            s = times((j + 1) * width, xh, xl, xh, xl, halves[j])
            rows = slice(0, (j + 1) * width)
            full[rows, halves[j]] = 2.25 * full[rows, halves[j]] - 1.5 * s
            for i in range(j + 1):
                keep(sh, sl, i, j, s[halves[i]])

    def cube():
        for j in (1, 0):
            rows = slice(0, (j + 1) * width)
            p = times((j + 1) * width, xh, xl, sh, sl, halves[j])
            full[rows, halves[j]] = full[rows, halves[j]] + 0.25 * p
        for i, j in upper:
            keep(xh, xl, i, j, full[halves[i], halves[j]])

    def turn():
        zmat[...] = 1.5 * zmat[...] - 0.5 * times(size, xh, xl, zh, zl, slice(None))
        zh[...], zl[...] = split(zmat[...])

    square()
    cube()

    def both(i, carry):
        square()
        turn()
        cube()
        return carry

    lax.fori_loop(1, ITERS - 1, both, 0)
    turn()

    factor = jnp.sqrt(rows_total / norm)
    top = zh[pl.ds(pl.multiple_of(core * width, width), width), :]
    low = zh[pl.ds(pl.multiple_of((1 - core) * width, width), width), :]
    zl[...] = jnp.concatenate([top, low], axis=0)
    for copy in loads:
        copy.wait()
    group = 4
    stores = []
    for i in range(tiles // group):
        at = pl.ds(i * group, group)
        a = own[at].reshape(group * TILE, width)
        b = par[at].reshape(group * TILE, width)
        value = jnp.dot(jnp.concatenate([a, b], axis=1), zl[...], preferred_element_type=F32)
        out[at] = (value * factor).astype(BF16).reshape(group, TILE, width)
        stores.append(pltpu.make_async_copy(out.at[at], out_hbm.at[at], out_sem.at[i]))
        stores[-1].start()
    for copy in stores:
        copy.wait()


def rotated(rows_total, gram, own, par):
    tiles, _, width = own.shape
    size = 2 * width
    any_space = pl.BlockSpec(memory_space=pl.ANY)
    vmem = pl.BlockSpec(memory_space=pltpu.VMEM)
    dma = pltpu.SemaphoreType.DMA
    return pl.pallas_call(
        functools.partial(rotate_kernel, rows_total),
        out_shape=jax.ShapeDtypeStruct(own.shape, BF16),
        in_specs=[vmem, any_space, any_space],
        out_specs=any_space,
        scratch_shapes=[
            pltpu.VMEM((size, size), F32),
            pltpu.VMEM((size, size), BF16),
            pltpu.VMEM((size, size), BF16),
            pltpu.VMEM((size, size), BF16),
            pltpu.VMEM((size, size), BF16),
            pltpu.VMEM((size, width), F32),
            pltpu.VMEM((size, width), BF16),
            pltpu.VMEM((size, width), BF16),
            pltpu.VMEM((tiles, TILE, width), BF16),
            pltpu.VMEM((tiles, TILE, width), BF16),
            pltpu.VMEM((tiles, TILE, width), BF16),
            dma((2,)),
            dma((tiles // 4,)),
        ],
        compiler_params=pltpu.CompilerParams(vmem_limit_bytes=48 * 2**20),
        name="rotate",
    )(gram, own, par)


def on_device(vectors, blocks, tile_cols, live_tiles):
    tiles, width = blocks.shape[0], vectors.shape[1]
    n_patch = lax.axis_size("patch")
    own, par, gram = filtered_and_gram(
        n_patch, vectors.reshape(tiles, TILE, width), blocks, tile_cols.T, live_tiles
    )
    result = rotated(n_patch * tiles * TILE, gram, own, par)
    return result.reshape(tiles * TILE, width)


def solution(mesh):
    in_specs = (P("patch", "cols"), P("patch", None, None, None), P("patch", None), P("patch"))
    out_specs = P("patch", "cols")
    return jax.shard_map(
        on_device, mesh=mesh, in_specs=in_specs, out_specs=out_specs, check_vma=False
    )
```

time: 77.2 us -> 71.3 us (0.924)
  Pallas kernels: 76.4 us -> 69.7 us
    pallas_call x1, Pallas kernels: 57.3 us -> 52.1 us  [filtered_and_gram(): pl.pallas_call(functools.partial(filter_kernel, n_patch), out_shape=(jax....]
    pallas_call x1, Pallas kernels: 19 us -> 17.5 us  [rotated(): pl.pallas_call(functools.partial(rotate_kernel, rows_total), out_shape=ja...]
where the time goes in v2:
time: 71.3 us; the launch traced here: 71.2 us
  Pallas kernels  69.7 us (98%)
  between operations  0.83 us (1%)
    pallas_call x1, Pallas kernels, filtered_and_gram(): pl.pallas_call(functools.partial(filter_kernel, n_patch), out_shape=(jax....  52.1 us
    pallas_call x1, Pallas kernels, rotated(): pl.pallas_call(functools.partial(rotate_kernel, rows_total), out_shape=ja...  17.5 us

profile of v2, /device:TPU:1, one launch (start us, length us, event | category | flops | bytes accessed | tf_op | source)
XLA Modules:
  0.0 71.2 jit_solution(8787057734388507277)
XLA Ops:
  0.7 0.0 copy-start
  0.7 0.7 copy-done
  1.3 52.1 %filter_gram.1 = (bf16[32,128,256]{2,1,0:T(8,128)(2,1)S(1)}, bf16[32,128,256]{2,1,0:T(8,128)(2,1)S(1)}, f32[2,16,33,128]{3,2,1,0:T(8,128)S(1)}) custom-call(s32[8,32]{1,0:T(8,128)S(1)} %bitcast.3, s32[1]{0:T(128)S(6)} %copy.5.live, bf16[32,128,256]{2,1,0:T(8,128)(2,1)} %bitcast.4, bf16[32,8,128,128]{3,2,1,0:T(8,128)(2,1)} %blk_hbm.1), custom_call_target="tpu_custom_call" | custom-call | tf_op jit(solution)/shard_map/filter_gram/pallas_call | solution.py:359
  53.5 17.5 %rotate.1 = bf16[32,128,256]{2,1,0:T(8,128)(2,1)} custom-call(f32[2,16,33,128]{3,2,1,0:T(8,128)S(1)} %get-tuple-element.8.gram, bf16[32,128,256]{2,1,0:T(8,128)(2,1)S(1)} %get-tuple-element.9.own_hbm, bf16[32,128,256]{2,1,0:T(8,128)(2,1)S(1)} %get-tuple-element.10.par_hbm), custom_call_target="tpu_custom_call" | custom-call | tf_op jit(solution)/shard_map/rotate/pallas_call | solution.py:537
Async XLA Ops:
  0.7 0.7 copy-start

commit v3 on v2

--- a/solution.py
+++ b/solution.py
@@ -14,6 +14,7 @@
 STEPS = 3
 ITERS = 8
 RING = 4
+GROUP = 4
 PIECES = 2
 SPLIT = 2
 
@@ -42,10 +43,10 @@
 
 
 def filter_kernel(
-    n_patch, cols, live, vec, blk_hbm, own_out, par_out, gram_out,
-    raw, blk, ys, los, his, par, acc, pay, rsb, zb, gb,
-    in_sem, blk_sem, halo_send, halo_recv, swap_send, swap_recv,
-    rs_send, rs_recv, z_send, z_recv, ag_send, ag_recv, gx_send, gx_recv, out_sem,
+    n_patch, cols_hbm, live, vec, blk_hbm, own_out, par_out, gram_out,
+    cols, raw, blk, ys, los, his, par, acc, pay, rsb, zb, tot,
+    in_sem, blk_sem, halo_send, halo_recv, core_send, core_recv, swap_recv,
+    plane_send, rs_recv, ag_recv, z_send, z_recv,
 ):
     tiles, width = raw.shape[0], raw.shape[2]
     part = width // SPLIT
@@ -96,6 +97,8 @@
     targets += [patch(z_peer(d)) for d in range(1, RING)]
     for target in targets:
         pl.semaphore_signal(barrier, inc=1, device_id=target, device_id_type=MESH)
+    list_load = pltpu.make_async_copy(cols_hbm, cols, in_sem.at[5])
+    list_load.start()
     for copy in loads[2:]:
         copy.start()
     blk_loads = [
@@ -150,8 +153,10 @@
         copy = send(
             mine[k][h].at[pl.ds(HALO + p * half, half)],
             theirs[k][h].at[pl.ds((0 if up else 2 * HALO) + p * half, half)],
-            halo_send.at[k, h, int(up), p], halo_recv.at[k, h, int(up), p], patch(right if up else left),
+            halo_send.at[h, int(up), p], halo_recv.at[k % 2, h, int(up), p], patch(right if up else left),
         )
+        if k > 0:
+            linked(up)(halos[k - 1, h, up, p].wait_send)
         linked(up)(copy.start)
         halos[k, h, up, p] = copy
 
@@ -206,7 +211,7 @@
         i = len(swaps)
         copy = send(
             ys[STEPS].at[pl.ds(start, count), :, lanes], par.at[pl.ds(start, count), :, lanes],
-            swap_send.at[i], swap_recv.at[i], {"cols": 1 - core},
+            core_send.at[i], swap_recv.at[i], {"cols": 1 - core},
         )
         copy.start()
         swaps.append(copy)
@@ -235,6 +240,7 @@
             if k == STEPS:
                 swap(first, HALO, lanes_of[h])
 
+    list_load.wait()
     inner(1, HALO, tiles - 2 * HALO, loading=True)
     for copy in (blk_loads[0], blk_loads[-1]):
         copy.wait()
@@ -258,22 +264,21 @@
         for h in range(SPLIT):
             outer(k, h)
         if k == 1:
+            for start in (HALO, tiles - edge):
+                inner(2, start, HALO)
+                copy_ends(2, start)
             inner(STEPS, HALO * STEPS, tiles - 2 * HALO * STEPS)
             swap(HALO * STEPS, tiles - 2 * HALO * STEPS, every)
-        for later in range(k + 1, STEPS + 1):
-            near = HALO * (later - k)
-            for start in (near, tiles - HALO - near):
-                inner(later, start, HALO)
-                if later == k + 1 and later < STEPS:
-                    copy_ends(later, start)
-                if later == STEPS:
-                    swap(start, HALO, every)
+        if k == 2:
+            for start in (2 * HALO, tiles - 3 * HALO, HALO, tiles - edge):
+                inner(STEPS, start, HALO)
+                swap(start, HALO, every)
         if k == STEPS - 1:
             early = len(swaps)
             for copy in swaps:
                 copy.wait_recv()
             gram(HALO, tiles - 2 * HALO, edge)
-    own_copy = pltpu.make_async_copy(ys[STEPS], own_out, out_sem.at[0])
+    own_copy = pltpu.make_async_copy(ys[STEPS], own_out, in_sem.at[0])
     own_copy.start()
 
     def ends(ref):
@@ -284,14 +289,14 @@
     acc[:, :width] += tdot(mine, mine)
     for copy in swaps[early:]:
         copy.wait_recv()
-    par_copy = pltpu.make_async_copy(par, par_out, out_sem.at[1])
+    par_copy = pltpu.make_async_copy(par, par_out, in_sem.at[1])
     par_copy.start()
     acc[:, width:] += tdot(ends(ys[STEPS]), ends(par))
     pack_gram(acc[:, :width], acc[:, width:], core == 0, pay)
 
     scatter = []
     for d in offsets:
-        copy = send(pay.at[peer_plane[d]], rsb.at[d], rs_send.at[d], rs_recv.at[d], patch(plane_peer(d)))
+        copy = send(pay.at[peer_plane[d]], rsb.at[d], plane_send.at[d - 1], rs_recv.at[d - 1], patch(plane_peer(d)))
         copy.start()
         scatter.append(copy)
     total = pay[plane]
@@ -301,9 +306,16 @@
     zb[z] = total
     along = []
     for d in range(1, RING):
-        copy = send(zb.at[z], zb.at[z], z_send.at[d], z_recv.at[d], patch(z_peer(d)))
+        copy = send(zb.at[z], zb.at[z], z_send.at[d - 1], z_recv.at[d - 1], patch(z_peer(d)))
         copy.start()
         along.append(copy)
+    for (k, h, up, p), copy in halos.items():
+        if k == STEPS - 1:
+            linked(up)(copy.wait_send)
+    for copy in swaps + scatter:
+        copy.wait_send()
+    own_copy.wait()
+    par_copy.wait()
     for copy in along:
         copy.wait_recv()
     total = zb[0]
@@ -311,36 +323,29 @@
         total = total + zb[d]
     for copy in along:
         copy.wait_send()
-    gb[core, plane] = total
+    tot[...] = total
     gather = []
     for d in offsets:
-        copy = send(
-            gb.at[core, plane], gb.at[core, plane], ag_send.at[d], ag_recv.at[d], patch(plane_peer(d))
-        )
+        copy = send(tot, gram_out.at[core, plane], plane_send.at[d - 1], ag_recv.at[d - 1], patch(plane_peer(d)))
         copy.start()
         gather.append(copy)
     across = []
 
-    def cross(d, at):
-        copy = send(gb.at[core, at], gb.at[core, at], gx_send.at[d], gx_recv.at[d], {"cols": 1 - core})
+    def cross(d, src, at):
+        copy = send(src, gram_out.at[core, at], core_send.at[d], core_recv.at[d], {"cols": 1 - core})
         copy.start()
         across.append(copy)
 
-    cross(0, plane)
+    cross(0, tot, plane)
+    gram_copy = pltpu.make_async_copy(tot, gram_out.at[core, plane], in_sem.at[2])
+    gram_copy.start()
     for d, copy in zip(offsets[::-1], gather[::-1]):
         copy.wait_recv()
-        cross(d, source_plane[d])
+        cross(d, gram_out.at[core, source_plane[d]], source_plane[d])
     for copy in across:
         copy.wait_recv()
-    gram_copy = pltpu.make_async_copy(gb, gram_out, out_sem.at[2])
-    gram_copy.start()
-
-    for (k, h, up, p), copy in halos.items():
-        linked(up)(copy.wait_send)
-    for copy in swaps + scatter + gather + across:
+    for copy in gather + across:
         copy.wait_send()
-    own_copy.wait()
-    par_copy.wait()
     gram_copy.wait()
 
 
@@ -355,7 +360,6 @@
     smem = pl.BlockSpec(memory_space=pltpu.SMEM)
     dma = pltpu.SemaphoreType.DMA
     side = [[pltpu.VMEM((3 * HALO, TILE, part), BF16) for _ in range(SPLIT)] for _ in range(STEPS)]
-    swaps = 2 * STEPS - 1 + 2 * SPLIT
     return pl.pallas_call(
         functools.partial(filter_kernel, n_patch),
         out_shape=(
@@ -363,9 +367,10 @@
             jax.ShapeDtypeStruct((tiles, TILE, width), BF16),
             jax.ShapeDtypeStruct((2, planes, chunk, TILE), F32),
         ),
-        in_specs=[smem, smem, hbm, hbm],
+        in_specs=[hbm, smem, hbm, hbm],
         out_specs=(any_space, any_space, any_space),
         scratch_shapes=[
+            pltpu.SMEM((nnz, tiles), jnp.int32),
             pltpu.VMEM((tiles, TILE, width), BF16),
             pltpu.VMEM((tiles, nnz, TILE, TILE), BF16),
             [pltpu.VMEM((tiles, TILE, width), BF16) for _ in range(STEPS + 1)],
@@ -376,22 +381,19 @@
             pltpu.VMEM((planes, chunk, TILE), F32),
             pltpu.VMEM((planes, chunk, TILE), F32),
             pltpu.VMEM((RING, chunk, TILE), F32),
-            pltpu.VMEM((2, planes, chunk, TILE), F32),
-            dma((5,)),
+            pltpu.VMEM((chunk, TILE), F32),
+            dma((6,)),
             dma((tiles // HALO,)),
-            dma((STEPS, SPLIT, 2, PIECES)),
-            dma((STEPS, SPLIT, 2, PIECES)),
-            dma((swaps,)),
-            dma((swaps,)),
+            dma((SPLIT, 2, PIECES)),
+            dma((2, SPLIT, 2, PIECES)),
             dma((planes,)),
             dma((planes,)),
-            dma((RING,)),
-            dma((RING,)),
-            dma((planes,)),
-            dma((planes,)),
-            dma((planes,)),
-            dma((planes,)),
-            dma((3,)),
+            dma((2 * STEPS - 1 + 2 * SPLIT,)),
+            dma((planes - 1,)),
+            dma((planes - 1,)),
+            dma((planes - 1,)),
+            dma((RING - 1,)),
+            dma((RING - 1,)),
         ],
         compiler_params=pltpu.CompilerParams(
             collective_id=0, has_side_effects=True, vmem_limit_bytes=48 * 2**20
@@ -401,15 +403,14 @@
 
 
 def rotate_kernel(
-    rows_total, gram, own_hbm, par_hbm, out_hbm, full, xh, xl, sh, sl, zmat, zh, zl, own, par, out, in_sem, out_sem
+    rows_total, gram, own_hbm, par_hbm, out_hbm, full, xh, xl, sh, sl, zmat, zh, zl, both_cores, out, in_sem, out_sem
 ):
-    width = own.shape[2]
+    _, tiles, _, width = both_cores.shape
     size = 2 * width
-    tiles = own.shape[0]
     core = lax.axis_index("cols")
     loads = [
-        pltpu.make_async_copy(own_hbm, own, in_sem.at[0]),
-        pltpu.make_async_copy(par_hbm, par, in_sem.at[1]),
+        pltpu.make_async_copy(own_hbm, both_cores.at[core], in_sem.at[0]),
+        pltpu.make_async_copy(par_hbm, both_cores.at[1 - core], in_sem.at[1]),
     ]
     for copy in loads:
         copy.start()
@@ -424,9 +425,9 @@
     blocks = {}
     for c in range(2):
         mixed, line = piece(c, 0), jnp.sum(gram[c, :, TILE // per :, :], axis=0)
-        turned = mixed.T
-        blocks[2 * c, 2 * c] = jnp.where(row <= lane, mixed, turned)
-        blocks[2 * c + 1, 2 * c + 1] = jnp.where(row > lane, mixed, jnp.where(row < lane, turned, line))
+        flipped = mixed.T
+        blocks[2 * c, 2 * c] = jnp.where(row <= lane, mixed, flipped)
+        blocks[2 * c + 1, 2 * c + 1] = jnp.where(row > lane, mixed, jnp.where(row < lane, flipped, line))
         blocks[2 * c, 2 * c + 1] = piece(c, 1)
     blocks[0, 2], blocks[1, 3] = piece(0, 2), piece(0, 3)
     blocks[2, 1], blocks[3, 0] = piece(1, 2), piece(1, 3)
@@ -492,8 +493,11 @@
         for i, j in upper:
             keep(xh, xl, i, j, full[halves[i], halves[j]])
 
+    def turned():
+        return 1.5 * zmat[...] - 0.5 * times(size, xh, xl, zh, zl, slice(None))
+
     def turn():
-        zmat[...] = 1.5 * zmat[...] - 0.5 * times(size, xh, xl, zh, zl, slice(None))
+        zmat[...] = turned()
         zh[...], zl[...] = split(zmat[...])
 
     square()
@@ -506,24 +510,30 @@
         return carry
 
     lax.fori_loop(1, ITERS - 1, both, 0)
-    turn()
-
+    zh[...] = turned().astype(BF16)
     factor = jnp.sqrt(rows_total / norm)
-    top = zh[pl.ds(pl.multiple_of(core * width, width), width), :]
-    low = zh[pl.ds(pl.multiple_of((1 - core) * width, width), width), :]
-    zl[...] = jnp.concatenate([top, low], axis=0)
     for copy in loads:
         copy.wait()
-    group = 4
+    group = GROUP
     stores = []
-    for i in range(tiles // group):
+
+    def product(i):
         at = pl.ds(i * group, group)
-        a = own[at].reshape(group * TILE, width)
-        b = par[at].reshape(group * TILE, width)
-        value = jnp.dot(jnp.concatenate([a, b], axis=1), zl[...], preferred_element_type=F32)
+        rows = [both_cores[c, at].reshape(group * TILE, width) for c in range(2)]
+        return jnp.dot(jnp.concatenate(rows, axis=1), zh[...], preferred_element_type=F32)
+
+    def finish(i, value):
+        at = pl.ds(i * group, group)
         out[at] = (value * factor).astype(BF16).reshape(group, TILE, width)
         stores.append(pltpu.make_async_copy(out.at[at], out_hbm.at[at], out_sem.at[i]))
         stores[-1].start()
+
+    value = product(0)
+    for i in range(1, tiles // group):
+        following = product(i)
+        finish(i - 1, value)
+        value = following
+    finish(tiles // group - 1, value)
     for copy in stores:
         copy.wait()
 
@@ -548,11 +558,10 @@
             pltpu.VMEM((size, width), F32),
             pltpu.VMEM((size, width), BF16),
             pltpu.VMEM((size, width), BF16),
-            pltpu.VMEM((tiles, TILE, width), BF16),
-            pltpu.VMEM((tiles, TILE, width), BF16),
+            pltpu.VMEM((2, tiles, TILE, width), BF16),
             pltpu.VMEM((tiles, TILE, width), BF16),
             dma((2,)),
-            dma((tiles // 4,)),
+            dma((tiles // GROUP,)),
         ],
         compiler_params=pltpu.CompilerParams(vmem_limit_bytes=48 * 2**20),
         name="rotate",
@@ -563,7 +572,8 @@
     tiles, width = blocks.shape[0], vectors.shape[1]
     n_patch = lax.axis_size("patch")
     own, par, gram = filtered_and_gram(
-        n_patch, vectors.reshape(tiles, TILE, width), blocks, tile_cols.T, live_tiles
+        n_patch, vectors.reshape(tiles, TILE, width), blocks,
+        pltpu.with_memory_space_constraint(tile_cols.T, pltpu.HBM), live_tiles,
     )
     result = rotated(n_patch * tiles * TILE, gram, own, par)
     return result.reshape(tiles * TILE, width)

time: 71.3 us -> 70 us (0.982)
  no operation moved by 1% of the time
where the time goes in v3:
time: 70 us; the launch traced here: 69.8 us
  Pallas kernels  69 us (99%)
  between operations  0.82 us (1%)
    pallas_call x1, Pallas kernels, filtered_and_gram(): pl.pallas_call(functools.partial(filter_kernel, n_patch), out_shape=(jax....  51.6 us
    pallas_call x1, Pallas kernels, rotated(): pl.pallas_call(functools.partial(rotate_kernel, rows_total), out_shape=ja...  17.4 us

profile of v3, /device:TPU:1, one launch (start us, length us, event | category | flops | bytes accessed | tf_op | source)
XLA Modules:
  0.0 69.8 jit_solution(18300825842354503981)
XLA Ops:
  0.7 51.6 %filter_gram.1 = (bf16[32,128,256]{2,1,0:T(8,128)(2,1)S(1)}, bf16[32,128,256]{2,1,0:T(8,128)(2,1)S(1)}, f32[2,16,33,128]{3,2,1,0:T(8,128)S(1)}) custom-call(s32[8,32]{1,0:T(8,128)} %bitcast.4, s32[1]{0:T(128)S(6)} %copy.5.live, bf16[32,128,256]{2,1,0:T(8,128)(2,1)} %bitcast.3, bf16[32,8,128,128]{3,2,1,0:T(8,128)(2,1)} %blk_hbm.1), custom_call_target="tpu_custom_call" | custom-call | tf_op jit(solution)/shard_map/filter_gram/pallas_call | solution.py:363
  52.2 17.4 %rotate.1 = bf16[32,128,256]{2,1,0:T(8,128)(2,1)} custom-call(f32[2,16,33,128]{3,2,1,0:T(8,128)S(1)} %get-tuple-element.8.gram, bf16[32,128,256]{2,1,0:T(8,128)(2,1)S(1)} %get-tuple-element.9.own_hbm, bf16[32,128,256]{2,1,0:T(8,128)(2,1)S(1)} %get-tuple-element.10.par_hbm), custom_call_target="tpu_custom_call" | custom-call | tf_op jit(solution)/shard_map/rotate/pallas_call | solution.py:547
